TPU v7x, 256 devices: a whole 4x4x8 slice. The times are simulated.
256 devices in a mesh: ind: 64 (over z_hi, y, x, core), snp: 4 (over z_lo).
Axes of the slice: x: 4, y: 4, z: 8 (z_hi: 2, z_lo: 4; z = z_hi * 4 + z_lo), core: 2. Of those that a mesh axis runs over, the one named last changes fastest.
Arguments:
- dosages: bfloat16 [11264, 131072], P('ind', 'snp'), may hold values from 0 to 2, as said below
- phenotype: int32 [11264], P('ind'), may hold values 0 or 1
- mean_effect: float32 [131072], P(('snp', 'ind')), may hold values from -3 to 3
- factor: float32 [131072, 256], P(('snp', 'ind')), may hold values from -1 to 1
- log_scale: float32 [131072], P(('snp', 'ind')), may hold values from -1 to 0
- diag_noise: float32 [131072, 128], P(('snp', 'ind')), may hold values from -5 to 5
- base_points: float32 [128, 256], replicated, may hold values from -5 to 5
Outputs:
- grad_mean: float32 [131072], P(('snp', 'ind'))
- grad_factor: float32 [131072, 256], P(('snp', 'ind'))
- grad_log_scale: float32 [131072], P(('snp', 'ind'))
- mean_loglik: float32 [], replicated
- rank_entropy: float32 [], replicated
Inputs may be any that keep to these rules, and one draw needn't show every extreme that they name: `dosages`: each entry is an allele count.
All inputs are finite; a program needn't handle non-finite values. No bound on the sum of `phenotype` on one device may be relied on, other than what follows from the above.
Results may differ from a plain program's by a relative error of at most 0.00085.
The roundings to bfloat16 on the way count: a program that leaves them out, or rounds other values in their place, can miss the bound.
Values may be sent and summed in bfloat16 or wider, within the bound.
No kernel may reach another device: no remote copies, remote signals or barrier semaphores. Data moves between devices by JAX's collectives and lax.ppermute only.
A program may use at most 128 MiB of HBM per device.

v0:
```python
import math
import jax
import jax.numpy as jnp
from jax import lax
from jax.sharding import PartitionSpec as P

P_SIZE = 131072
R = 256
S = 128
COHORT_RATIO = 40


def invert_gram(gram_matrix):
    factor_chol = jnp.linalg.cholesky(gram_matrix)
    identity = jnp.eye(gram_matrix.shape[0], dtype=gram_matrix.dtype)
    lower_inv = lax.linalg.triangular_solve(factor_chol, identity, left_side=True, lower=True)
    inverse = jnp.dot(lower_inv.T, lower_inv, precision=lax.Precision.HIGHEST)
    return (factor_chol, inverse)


def on_device(dosages, phenotype, mean_effect, factor, log_scale, diag_noise, base_points):
    sample_count = base_points.shape[0]
    local_ind = dosages.shape[0]
    total_ind = local_ind * lax.axis_size("ind")
    root_p = math.sqrt(P_SIZE)
    spread = jnp.exp(log_scale)
    low_rank = jnp.dot(factor, base_points.T, precision=lax.Precision.HIGHEST)
    samples = ((mean_effect[:, None] + low_rank + spread[:, None] * diag_noise) / root_p).astype(
        jnp.bfloat16
    )
    columns = dosages
    partial_logits = jnp.dot(
        columns,
        lax.all_gather(samples, "ind", axis=0, tiled=True),
        preferred_element_type=jnp.float32,
    )
    labels = phenotype.astype(jnp.float32)[:, None]
    logits = lax.psum(partial_logits.astype(jnp.bfloat16), "snp").astype(jnp.float32)
    loglik_terms = jnp.sum(labels * logits - jax.nn.softplus(logits))
    loglik_total = lax.psum(loglik_terms, "ind")
    weights = (COHORT_RATIO * (labels - jax.nn.sigmoid(logits)) / S).astype(jnp.bfloat16)
    mean_loglik = loglik_total / (total_ind * sample_count)
    columns = dosages
    gradient = lax.psum_scatter(
        lax.dot_general(
            columns, weights, (((0,), (0,)), ((), ())), preferred_element_type=jnp.float32
        ),
        "ind",
        scatter_dimension=0,
        tiled=True,
    )
    scaled = factor / spread[:, None]
    identity = jnp.eye(R, dtype=jnp.float32)
    gram_part = jnp.dot(scaled.T, scaled, precision=lax.Precision.HIGHEST)
    gram_matrix = identity + lax.psum(gram_part, ("ind", "snp"))
    factor_chol, inverse = invert_gram(gram_matrix)
    rank_entropy = jnp.sum(jnp.log(jnp.diagonal(factor_chol))) / R
    projected = jnp.dot(factor, inverse, precision=lax.Precision.HIGHEST)
    spread_sq = spread * spread
    grad_mean = jnp.sum(gradient, axis=1) / root_p - mean_effect
    grad_factor = (
        jnp.dot(gradient, base_points, precision=lax.Precision.HIGHEST) / root_p
        - factor
        + projected / spread_sq[:, None]
    )
    leverage = jnp.sum(projected * factor, axis=1)
    grad_log_scale = (
        spread * jnp.sum(gradient * diag_noise, axis=1) / root_p
        + 1.0
        - spread_sq
        - leverage / spread_sq
    )
    return (grad_mean, grad_factor, grad_log_scale, mean_loglik, rank_entropy)


def solution(mesh):
    in_specs = (
        P("ind", "snp"),
        P("ind"),
        P(("snp", "ind")),
        P(("snp", "ind"), None),
        P(("snp", "ind")),
        P(("snp", "ind"), None),
        P(),
    )
    out_specs = (P(("snp", "ind")), P(("snp", "ind"), None), P(("snp", "ind")), P(), P())
    return jax.shard_map(
        on_device, mesh=mesh, in_specs=in_specs, out_specs=out_specs, check_vma=False
    )
```

profile of v0, /device:TPU:32, one launch (start us, length us, event | category | flops | bytes accessed | tf_op | source)
XLA Modules:
  0.0 618.1 jit_solution(5039435738711736244)
XLA Ops:
  8.0 0.0 copy-start
  8.0 0.0 all-gather.2.cloned.1.call-start
  8.1 0.7 exp.10
  8.8 0.1 copy-done
  8.9 2.4 fusion.4
  11.3 0.0 all-gather.2.cloned.1.call-update
  11.3 0.0 all-reduce.3.cloned.1.call-start
  11.3 3.1 fusion.6
  14.4 0.0 all-reduce.3.cloned.1.call-update
  14.4 0.0 reduce-scatter.2.cloned.1.call-start
  14.5 0.7 convert_element_type.24
  15.2 112.5 %all-gather.2.cloned.1.call-done = bf16[32768,128]{1,0:T(8,128)(2,1)} async-done(((bf16[512,128]{1,0:T(8,128)(2,1)}), bf16[32768,128]{1,0:T(8,128)(2,1)}) %all-gather.2.cloned.1.call-update) | async-done | bytes 8388624 | tf_op jit(solution)/shard_map/all_gather | solution.py:34
  127.6 9.9 %fusion.5 = bf16[176,128]{1,0:T(8,128)(2,1)S(1)} fusion(bf16[176,32768]{1,0:T(8,128)(2,1)} %param.7, bf16[32768,128]{1,0:T(8,128)(2,1)} %all-gather.2.cloned.1.call-done), kind=kOutput, calls=%fused_computation.15 | convolution fusion | flops 1476417536 | bytes 19968000 | tf_op jit(solution)/shard_map/dot_general | solution.py:32
  137.5 15.6 %psum.21 = bf16[176,128]{1,0:T(8,128)(2,1)S(1)} all-reduce(bf16[176,128]{1,0:T(8,128)(2,1)S(1)} %fusion.5), channel_id=1, replica_groups=mesh['ind'=64,'snp'=4] {'snp'}, use_global_device_ids=true, to_apply=%region_0.0 | all-reduce | flops 22528 | bytes 90112 | tf_op jit(solution)/shard_map/psum | solution.py:38
  153.1 12.5 %convolution_bitcast_fusion = f32[32768,128]{0,1:T(8,128)} fusion(bf16[176,32768]{1,0:T(8,128)(2,1)} %param.7, bf16[176,128]{1,0:T(8,128)(2,1)S(1)} %psum.21, f32[176]{0:T(256)S(1)} %convert_element_type.24), kind=kOutput, calls=%fused_computation.3 | convolution fusion | flops 1476552704 | bytes 28357312 | tf_op jit(solution)/shard_map/dot_general | solution.py:45
  165.6 0.0 copy-start.2
  165.6 0.0 copy-start.1
  165.6 0.0 copy-start.3
  165.6 0.0 copy-start.4
  165.6 0.0 reduce-scatter.2.cloned.1.call-update
  165.6 0.9 copy-done.2
  166.5 0.1 copy.19
  166.7 122.0 %all-reduce.3.cloned.1.call-done = f32[256,256]{0,1:T(8,128)} async-done(((f32[256,256]{0,1:T(8,128)}), f32[256,256]{0,1:T(8,128)}) %all-reduce.3.cloned.1.call-update) | async-done | bytes 262160 | tf_op jit(solution)/shard_map/psum | solution.py:55
  288.7 1.0 convert_add_fusion
  289.7 0.1 copy.17
  289.8 1.0 fusion.12
  290.8 11.7 %cholesky.50 = f32[128,128]{1,0:T(8,128)S(1)} custom-call(f32[128,128]{1,0:T(8,128)S(1)} %cholesky.118), custom_call_target="Cholesky" | custom-call | tf_op jit(solution)/shard_map/jit(cholesky)/cholesky | solution.py:14
  302.6 9.8 %custom-call.14 = f32[1,128,128]{1,2,0:T(8,128)S(1)} custom-call(f32[1,128,128]{2,1,0:T(8,128)S(1)} %get-tuple-element.30), custom_call_target="InvertDiagBlocksLowerTriangular" | custom-call | tf_op jit(solution)/shard_map/jit(cholesky)/cholesky | solution.py:14
  312.4 0.2 constant_dynamic-update-slice_fusion.1
  312.6 0.3 convolution_subtract_fusion.1
  312.9 11.9 %cholesky.105 = f32[128,128]{1,0:T(8,128)S(1)} custom-call(f32[128,128]{1,0:T(8,128)S(1)} %convolution_subtract_fusion.1), custom_call_target="Cholesky" | custom-call | tf_op jit(solution)/shard_map/jit(cholesky)/cholesky | solution.py:14
  324.8 0.6 compare_reduce_fusion.1
  325.5 0.6 compare_reduce_fusion
  327.5 0.1 triangular_solve.64
  327.5 4.0 while.1
  327.5 0.6 fusion.57
  328.1 1.4 bitcast_dynamic-update-slice_fusion.2
  329.5 0.6 fusion.57
  330.1 1.4 bitcast_dynamic-update-slice_fusion.2
  331.5 19.7 %custom-call.15 = f32[2,128,128]{1,2,0:T(8,128)S(1)} custom-call(f32[2,128,128]{2,1,0:T(8,128)S(1)} %get-tuple-element.12), custom_call_target="InvertDiagBlocksLowerTriangular" | custom-call | tf_op jit(solution)/shard_map/triangular_solve | solution.py:16
  351.2 2.3 gather_fusion
  353.6 0.6 log_reduce_fusion
  354.2 0.3 fusion.15
  354.4 0.4 convolution_subtract_fusion
  354.8 0.3 fusion.31
  355.1 0.6 fusion.8
  355.8 0.0 copy-done.1
  355.8 0.7 multiply_reduce_fusion
  356.4 0.7 fusion.25
  357.8 208.4 %psum.23 = f32[]{:T(128)} all-reduce(f32[]{:T(128)} %fusion.25), channel_id=1, replica_groups=mesh['ind'=64,'snp'=4] {'ind'}, use_global_device_ids=true, to_apply=%region_11.12 | all-reduce | flops 1 | bytes 8 | tf_op jit(solution)/shard_map/psum | solution.py:40
  566.9 37.5 %reduce-scatter.2.cloned.1.call-done = f32[512,128]{0,1:T(8,128)} async-done(((f32[32768,128]{0,1:T(8,128)}), f32[512,128]{0,1:T(8,128)}) %reduce-scatter.2.cloned.1.call-update) | async-done | bytes 262160 | tf_op jit(solution)/shard_map/reduce_scatter | solution.py:44
  604.4 1.0 multiply_reduce_fusion.1
  605.4 0.0 copy-done.3
  605.4 0.0 copy-done.4
  605.4 0.6 divide_subtract_fusion
  606.0 2.4 fusion.1
  (12 shorter events, 0.2 us)
Async XLA Ops:
  8.0 0.9 copy-start
  8.0 119.6 %all-gather.2.cloned.1.call-start = ((), (), s32[]{:S(2)}) async-start(), calls=%async_computation.1 | async-start | bytes 8519680 | tf_op jit(solution)/shard_map/all_gather | solution.py:34
  11.3 277.4 %all-reduce.3.cloned.1.call-start = ((), (), s32[]{:S(2)}) async-start(), calls=%async_computation.3 | async-start | bytes 524288 | tf_op jit(solution)/shard_map/psum | solution.py:55
  14.4 589.9 %reduce-scatter.2.cloned.1.call-start = ((), (), s32[]{:S(2)}) async-start(), calls=%async_computation.2 | async-start | bytes 17039360 | tf_op jit(solution)/shard_map/reduce_scatter | solution.py:44
  165.6 0.9 copy-start.2
  165.6 190.2 %copy-start.1 = (f32[512,256]{1,0:T(8,128)S(1)}, f32[512,256]{1,0:T(8,128)}, u32[]{:S(2)}) copy-start(f32[512,256]{1,0:T(8,128)} %param.10) | copy-start | bytes 1572868
  165.6 439.8 %copy-start.3 = (f32[512]{0:T(512)S(1)}, f32[512]{0:T(512)}, u32[]{:S(2)}) copy-start(f32[512]{0:T(512)} %param.9) | copy-start | bytes 6148
  165.6 439.8 %copy-start.4 = (f32[512]{0:T(512)S(1)}, f32[512]{0:T(512)}, u32[]{:S(2)}) copy-start(f32[512]{0:T(512)} %param.11) | copy-start | bytes 6148
Sparse Core Ops, SparseCore 0:
  12.5 115.0 all-gather.1
  165.7 438.5 reduce-scatter.1
Sparse Core Ops, SparseCore 1:
  17.8 270.9 all-reduce.2
where the time goes:
time: 619 us; the launch traced here: 618 us
  waiting for transfers between devices  272 us (44%)
  blocking collectives  224 us (36%)
  other arithmetic  60.1 us (10%)
  matrix products  32.9 us (5%)
  between operations  20.6 us (3%)
  local copies, waits for them, and re-layouts  8.42 us (1%)
    psum x1, blocking collectives, on_device(): loglik_total = lax.psum(loglik_terms, 'ind')  208 us
    psum x1, waiting for transfers between devices, on_device(): gram_matrix = identity + lax.psum(gram_part, ('ind', 'snp'))  122 us
    all_gather x1, waiting for transfers between devices, on_device(): lax.all_gather(samples, 'ind', axis=0, tiled=True)  112 us
    reduce_scatter x1, waiting for transfers between devices, on_device(): lax.psum_scatter(lax.dot_general(columns, weights, (((0,), (0,)), ((), ()...  37.5 us
    another operation x7, other arithmetic, invert_gram(): factor_chol = jnp.linalg.cholesky(gram_matrix)  34.8 us
    another operation x3, other arithmetic, invert_gram(): lax.linalg.triangular_solve(factor_chol, identity, left_side=True, lower=...  19.7 us
    psum x1, blocking collectives, on_device(): lax.psum(partial_logits.astype(jnp.bfloat16), 'snp').astype(jnp.float32)  15.6 us
    dot_general x1, matrix products, on_device(): lax.dot_general(columns, weights, (((0,), (0,)), ((), ())), preferred_ele...  12.5 us
  transfers between devices with their start and end apart: 3, of which 3 were waited for; matrix products, arithmetic and copies ran while one was open for 15% of the time, Pallas kernels for 0%

commit v1 on v0

--- a/solution.py
+++ b/solution.py
@@ -31,7 +31,9 @@
     columns = dosages
     partial_logits = jnp.dot(
         columns,
-        lax.all_gather(samples, "ind", axis=0, tiled=True),
+        jnp.concatenate(
+            lax.all_to_all(jnp.stack([samples] * lax.axis_size("ind")), "ind", 0, 0), axis=0
+        ),
         preferred_element_type=jnp.float32,
     )
     labels = phenotype.astype(jnp.float32)[:, None]

time: 619 us -> 741 us (1.20)
  waiting for transfers between devices: 272 us -> 364 us
  blocking collectives: 224 us -> 238 us
  starting transfers between devices: 0.12 us -> 14.1 us
    all_to_all x0 -> x1, waiting for transfers between devices: none -> 184 us  [on_device(): lax.all_to_all(jnp.stack([samples] * lax.axis_size('ind')), 'ind', 0, 0)]
    all_gather x1 -> x0, waiting for transfers between devices: 112 us -> none  [on_device(): lax.all_gather(samples, 'ind', axis=0, tiled=True)]
    psum x1, waiting for transfers between devices: 122 us -> 180 us  [on_device(): gram_matrix = identity + lax.psum(gram_part, ('ind', 'snp'))]
    reduce_scatter x1, waiting for transfers between devices: 37.5 us -> 0.03 us  [on_device(): lax.psum_scatter(lax.dot_general(columns, weights, (((0,), (0,)), ((), ()...]
    all_to_all x0 -> x1, starting transfers between devices: none -> 14.1 us  [on_device(): lax.all_to_all(jnp.stack([samples] * lax.axis_size('ind')), 'ind', 0, 0)]
    psum x1, blocking collectives: 15.6 us -> 27.3 us  [on_device(): lax.psum(partial_logits.astype(jnp.bfloat16), 'snp').astype(jnp.float32)]
  transfers between devices with their start and end apart: 3 -> 3, of which waited for: 3 -> 2; matrix products, arithmetic and copies ran while one was open for 15% -> 12% of each run, Pallas kernels for 0% -> 0%
where the time goes in v1:
time: 741 us
  waiting for transfers between devices  364 us (49%)
  blocking collectives  238 us (32%)
  other arithmetic  59.4 us (8%)
  matrix products  30.9 us (4%)
  between operations  20.6 us (3%)
  starting transfers between devices  14.1 us (2%)
  local copies, waits for them, and re-layouts  13.7 us (2%)
    psum x1, blocking collectives, on_device(): loglik_total = lax.psum(loglik_terms, 'ind')  211 us
    all_to_all x1, waiting for transfers between devices, on_device(): lax.all_to_all(jnp.stack([samples] * lax.axis_size('ind')), 'ind', 0, 0)  184 us
    psum x1, waiting for transfers between devices, on_device(): gram_matrix = identity + lax.psum(gram_part, ('ind', 'snp'))  180 us
    another operation x7, other arithmetic, invert_gram(): factor_chol = jnp.linalg.cholesky(gram_matrix)  34.8 us
    psum x1, blocking collectives, on_device(): lax.psum(partial_logits.astype(jnp.bfloat16), 'snp').astype(jnp.float32)  27.3 us
    another operation x3, other arithmetic, invert_gram(): lax.linalg.triangular_solve(factor_chol, identity, left_side=True, lower=...  19.7 us
  transfers between devices with their start and end apart: 3, of which 2 were waited for; matrix products, arithmetic and copies ran while one was open for 12% of the time, Pallas kernels for 0%

profile of v1, /device:TPU:32, one launch (start us, length us, event | category | flops | bytes accessed | tf_op | source)
XLA Modules:
  0.0 741.0 jit_solution(7549831057229343768)
XLA Ops:
  8.0 0.0 copy-start
  8.0 0.7 exp.10
  8.7 0.2 copy-done
  8.9 1.7 fusion.4
  10.6 0.0 copy-start.1
  10.6 5.2 stack.2
  15.9 0.0 copy-start.5
  15.9 14.1 %all-to-all-start = ((bf16[64,512,128]{2,1,0:T(8,128)(2,1)}), bf16[64,512,128]{2,1,0:T(8,128)(2,1)}, u32[]{:S(2)}, u32[]{:S(2)}) async-start(bf16[64,512,128]{2,1,0:T(8,128)(2,1)} %stack.2), calls=%async_computation | async-start | bytes 16777216 | tf_op jit(solution)/shard_map/all_to_all | solution.py:35
  30.0 0.0 all-reduce.3.cloned.1.call-start
  30.0 0.0 copy-done.1
  30.0 1.9 fusion.6
  31.9 0.0 all-reduce.3.cloned.1.call-update
  31.9 0.0 reduce-scatter.2.cloned.1.call-start
  32.0 0.0 copy-done.5
  32.0 184.0 %all-to-all-done = bf16[64,512,128]{2,1,0:T(8,128)(2,1)} async-done(((bf16[64,512,128]{2,1,0:T(8,128)(2,1)}), bf16[64,512,128]{2,1,0:T(8,128)(2,1)}, u32[]{:S(2)}, u32[]{:S(2)}) %all-to-all-start) | async-done | bytes 8388640 | tf_op jit(solution)/shard_map/all_to_all | solution.py:35
  216.0 9.8 %fusion.5 = bf16[176,128]{1,0:T(8,128)(2,1)S(1)} fusion(bf16[176,32768]{1,0:T(8,128)(2,1)} %param.7, bf16[32768,128]{1,0:T(8,128)(2,1)} %bitcast), kind=kOutput, calls=%fused_computation.15 | convolution fusion | flops 1476417536 | bytes 19968000 | tf_op jit(solution)/shard_map/dot_general | solution.py:32
  225.9 27.3 %psum.21 = bf16[176,128]{1,0:T(8,128)(2,1)S(1)} all-reduce(bf16[176,128]{1,0:T(8,128)(2,1)S(1)} %fusion.5), channel_id=1, replica_groups=mesh['ind'=64,'snp'=4] {'snp'}, use_global_device_ids=true, to_apply=%region_0.0 | all-reduce | flops 22528 | bytes 90112 | tf_op jit(solution)/shard_map/psum | solution.py:40
  253.2 12.4 %convolution_bitcast_fusion = f32[32768,128]{0,1:T(8,128)} fusion(bf16[176,32768]{1,0:T(8,128)(2,1)} %param.7, bf16[176,128]{1,0:T(8,128)(2,1)S(1)} %psum.21, f32[176]{0:T(256)S(1)} %convert_element_type.24), kind=kOutput, calls=%fused_computation.3 | convolution fusion | flops 1476552704 | bytes 28357312 | tf_op jit(solution)/shard_map/dot_general | solution.py:47
  265.6 0.0 copy-start.2
  265.6 0.0 copy-start.3
  265.6 0.0 copy-start.4
  265.6 0.0 reduce-scatter.2.cloned.1.call-update
  265.7 0.9 copy-done.2
  266.6 0.1 copy.19
  266.8 180.1 %all-reduce.3.cloned.1.call-done = f32[256,256]{0,1:T(8,128)} async-done(((f32[256,256]{0,1:T(8,128)}), f32[256,256]{0,1:T(8,128)}) %all-reduce.3.cloned.1.call-update) | async-done | bytes 262160 | tf_op jit(solution)/shard_map/psum | solution.py:57
  446.9 1.0 convert_add_fusion
  447.9 0.1 copy.17
  448.1 1.0 fusion.12
  449.1 11.7 %cholesky.50 = f32[128,128]{1,0:T(8,128)S(1)} custom-call(f32[128,128]{1,0:T(8,128)S(1)} %cholesky.118), custom_call_target="Cholesky" | custom-call | tf_op jit(solution)/shard_map/jit(cholesky)/cholesky | solution.py:14
  460.8 9.8 %custom-call.14 = f32[1,128,128]{1,2,0:T(8,128)S(1)} custom-call(f32[1,128,128]{2,1,0:T(8,128)S(1)} %get-tuple-element.30), custom_call_target="InvertDiagBlocksLowerTriangular" | custom-call | tf_op jit(solution)/shard_map/jit(cholesky)/cholesky | solution.py:14
  470.7 0.2 constant_dynamic-update-slice_fusion.1
  470.9 0.3 convolution_subtract_fusion.1
  471.1 11.9 %cholesky.105 = f32[128,128]{1,0:T(8,128)S(1)} custom-call(f32[128,128]{1,0:T(8,128)S(1)} %convolution_subtract_fusion.1), custom_call_target="Cholesky" | custom-call | tf_op jit(solution)/shard_map/jit(cholesky)/cholesky | solution.py:14
  483.1 0.6 compare_reduce_fusion.1
  483.7 0.6 compare_reduce_fusion
  485.7 0.1 triangular_solve.64
  485.8 4.0 while.1
  485.8 0.6 fusion.57
  486.4 1.4 bitcast_dynamic-update-slice_fusion.2
  487.8 0.6 fusion.57
  488.4 1.4 bitcast_dynamic-update-slice_fusion.2
  489.8 19.7 %custom-call.15 = f32[2,128,128]{1,2,0:T(8,128)S(1)} custom-call(f32[2,128,128]{2,1,0:T(8,128)S(1)} %get-tuple-element.12), custom_call_target="InvertDiagBlocksLowerTriangular" | custom-call | tf_op jit(solution)/shard_map/triangular_solve | solution.py:16
  509.5 2.3 gather_fusion
  511.8 0.6 log_reduce_fusion
  512.4 0.3 fusion.15
  512.7 0.4 convolution_subtract_fusion
  513.1 0.3 fusion.31
  513.4 0.6 fusion.8
  514.0 0.7 multiply_reduce_fusion
  514.7 0.7 fusion.25
  516.0 210.5 %psum.23 = f32[]{:T(128)} all-reduce(f32[]{:T(128)} %fusion.25), channel_id=1, replica_groups=mesh['ind'=64,'snp'=4] {'ind'}, use_global_device_ids=true, to_apply=%region_11.12 | all-reduce | flops 1 | bytes 8 | tf_op jit(solution)/shard_map/psum | solution.py:42
  727.2 0.0 reduce-scatter.2.cloned.1.call-done
  727.3 1.0 multiply_reduce_fusion.1
  728.3 0.0 copy-done.3
  728.3 0.0 copy-done.4
  728.3 0.6 divide_subtract_fusion
  728.9 2.4 fusion.1
  (13 shorter events, 0.2 us)
Async XLA Ops:
  8.0 0.9 copy-start
  10.6 19.4 %copy-start.1 = (f32[512,256]{1,0:T(8,128)S(1)}, f32[512,256]{1,0:T(8,128)}, u32[]{:S(2)}) copy-start(f32[512,256]{1,0:T(8,128)} %param.10) | copy-start | bytes 1572868
  15.9 16.1 %copy-start.5 = (s32[176]{0:T(256)S(1)}, s32[176]{0:T(256)}, u32[]{:S(2)}) copy-start(s32[176]{0:T(256)} %param.8) | copy-start | bytes 2116
  15.9 200.1 %all-to-all-start = ((bf16[64,512,128]{2,1,0:T(8,128)(2,1)}), bf16[64,512,128]{2,1,0:T(8,128)(2,1)}, u32[]{:S(2)}, u32[]{:S(2)}) async-start(bf16[64,512,128]{2,1,0:T(8,128)(2,1)} %stack.2), calls=%async_computation | async-start | bytes 16777216 | tf_op jit(solution)/shard_map/all_to_all | solution.py:35
  30.0 417.0 %all-reduce.3.cloned.1.call-start = ((), (), s32[]{:S(2)}) async-start(), calls=%async_computation.3 | async-start | bytes 524288 | tf_op jit(solution)/shard_map/psum | solution.py:57
  31.9 695.3 %reduce-scatter.2.cloned.1.call-start = ((), (), s32[]{:S(2)}) async-start(), calls=%async_computation.2 | async-start | bytes 17039360 | tf_op jit(solution)/shard_map/reduce_scatter | solution.py:46
  265.6 0.9 copy-start.2
  265.6 462.6 %copy-start.3 = (f32[512]{0:T(512)S(1)}, f32[512]{0:T(512)}, u32[]{:S(2)}) copy-start(f32[512]{0:T(512)} %param.9) | copy-start | bytes 6148
  265.6 462.6 %copy-start.4 = (f32[512]{0:T(512)S(1)}, f32[512]{0:T(512)}, u32[]{:S(2)}) copy-start(f32[512]{0:T(512)} %param.11) | copy-start | bytes 6148
Sparse Core Ops, SparseCore 0:
  36.8 410.0 all-reduce.2
Sparse Core Ops, SparseCore 1:
  265.8 443.0 reduce-scatter.1
